TPU v7x, 256 devices: a whole 4x4x8 slice. The times are simulated.
256 devices in a mesh: dp: 16 (over x, y_hi, core), fsdp: 16 (over y_lo, z).
Axes of the slice: x: 4, y: 4 (y_hi: 2, y_lo: 2; y = y_hi * 2 + y_lo), z: 8, core: 2. Of those that a mesh axis runs over, the one named last changes fastest.
Arguments:
- tokens: bfloat16 [8192, 2048], P('dp'), may hold values from -6 to 6
- expert_ids: int32 [8192, 2], P('dp'), may hold values from 0 to 7, as said below
- route_probs: float32 [8192, 2], P('dp'), may hold values from 0.1 to 1
- gate_w: bfloat16 [2, 2048, 7168], P(None, 'dp', 'fsdp'), may hold values from -0.125 to 0.125
- up_w: bfloat16 [2, 2048, 7168], P(None, 'dp', 'fsdp'), may hold values from -0.125 to 0.125
- down_w: bfloat16 [2, 7168, 2048], P(None, 'fsdp', 'dp'), may hold values from -0.0625 to 0.0625
- out_grad: bfloat16 [8192, 2048], P('dp'), may hold values from -6 to 6
Outputs:
- mixed: bfloat16 [8192, 2048], P('dp')
- token_grad: bfloat16 [8192, 2048], P('dp')
- gate_grad: bfloat16 [2, 2048, 7168], P(None, 'dp', 'fsdp')
- up_grad: bfloat16 [2, 2048, 7168], P(None, 'dp', 'fsdp')
- down_grad: bfloat16 [2, 7168, 2048], P(None, 'fsdp', 'dp')
Inputs may be any that keep to these rules, and one draw needn't show every extreme that they name: `expert_ids`: the two entries of a row differ. In each aligned block of 512 rows (the rows of one index of dp) every expert is named by at most 256 rows, and one of experts 0 to 1 by exactly 256 rows.
All inputs are finite; a program needn't handle non-finite values.
Results may differ from a plain program's by a relative error of at most 0.018.
Values may be sent and summed in bfloat16 or wider, within the bound.
A program may use at most 128 MiB of HBM per device.

v0:
```python
import jax
import jax.numpy as jnp
from jax import lax
from jax.sharding import PartitionSpec as P


def slot_layout(expert_ids, route_probs, expert, slot_cap):
    token_count = expert_ids.shape[0]
    matches = expert_ids == expert
    chosen = jnp.any(matches, axis=1)
    weight_token = jnp.sum(jnp.where(matches, route_probs, jnp.float32(0.0)), axis=1)
    position = jnp.cumsum(chosen.astype(jnp.int32)) - 1
    slot_index = lax.broadcasted_iota(jnp.int32, (slot_cap, token_count), 0)
    token_index = lax.broadcasted_iota(jnp.int32, (slot_cap, token_count), 1)
    matched_slots = (position[None, :] == slot_index) & chosen[None, :]
    slot_token = jnp.sum(jnp.where(matched_slots, token_index, 0), axis=1)
    slot_valid = jnp.any(matched_slots, axis=1)
    slot_weight = jnp.where(slot_valid, jnp.take(weight_token, slot_token), jnp.float32(0.0))
    token_slot = jnp.clip(position, 0, slot_cap - 1)
    return (chosen, token_slot, slot_token, slot_valid, slot_weight)


def group_total(partial_value):
    return lax.psum(partial_value.astype(jnp.bfloat16), "fsdp")


def body(tokens, expert_ids, route_probs, gate_w, up_w, down_w, out_grad):
    token_count = tokens.shape[0]
    width = tokens.shape[1]
    slot_cap = token_count // 2
    window = gate_w.shape[0]
    mixed_part = jnp.zeros((token_count, width), jnp.float32)
    stored = []
    for expert in range(window):
        chosen, token_slot, slot_token, slot_valid, slot_weight = slot_layout(
            expert_ids, route_probs, expert, slot_cap
        )
        gate_full, up_full, down_full = (
            lax.all_gather(gate_w[expert], "dp", axis=0, tiled=True),
            lax.all_gather(up_w[expert], "dp", axis=0, tiled=True),
            lax.all_gather(down_w[expert], "dp", axis=1, tiled=True),
        )
        slot_input = jnp.take(tokens, slot_token, axis=0) * slot_valid[:, None].astype(tokens.dtype)
        gate_act = jnp.dot(slot_input, gate_full, preferred_element_type=jnp.float32)
        up_act = jnp.dot(slot_input, up_full, preferred_element_type=jnp.float32)
        hidden = (jax.nn.silu(gate_act) * up_act).astype(jnp.bfloat16)
        expert_out = (
            jnp.dot(hidden, down_full, preferred_element_type=jnp.float32) * slot_weight[:, None]
        )
        mixed_part = mixed_part + jnp.where(
            chosen[:, None], jnp.take(expert_out, token_slot, axis=0), jnp.float32(0.0)
        )
        stored.append(
            (
                chosen,
                token_slot,
                slot_token,
                slot_weight,
                slot_input,
                gate_act,
                up_act,
                hidden,
                gate_full,
                up_full,
                down_full,
            )
        )
    mixed = group_total(mixed_part)
    grad_part = jnp.zeros((token_count, width), jnp.float32)
    gate_grads, up_grads, down_grads = ([], [], [])
    for expert in range(window):
        (
            chosen,
            token_slot,
            slot_token,
            slot_weight,
            slot_input,
            gate_act,
            up_act,
            hidden,
            gate_full,
            up_full,
            down_full,
        ) = stored[expert]
        slot_grad = (
            jnp.take(out_grad, slot_token, axis=0).astype(jnp.float32) * slot_weight[:, None]
        ).astype(jnp.bfloat16)
        down_term = lax.dot_general(
            hidden, slot_grad, (((0,), (0,)), ((), ())), preferred_element_type=jnp.float32
        )
        hidden_grad = lax.dot_general(
            slot_grad, down_full, (((1,), (1,)), ((), ())), preferred_element_type=jnp.float32
        )
        sigma = jax.nn.sigmoid(gate_act)
        up_act_grad = (hidden_grad * gate_act * sigma).astype(jnp.bfloat16)
        gate_act_grad = (hidden_grad * up_act * sigma * (1.0 + gate_act * (1.0 - sigma))).astype(
            jnp.bfloat16
        )
        gate_term = lax.dot_general(
            slot_input, gate_act_grad, (((0,), (0,)), ((), ())), preferred_element_type=jnp.float32
        )
        up_term = lax.dot_general(
            slot_input, up_act_grad, (((0,), (0,)), ((), ())), preferred_element_type=jnp.float32
        )
        input_grad = lax.dot_general(
            gate_act_grad, gate_full, (((1,), (1,)), ((), ())), preferred_element_type=jnp.float32
        )
        input_grad = input_grad + lax.dot_general(
            up_act_grad, up_full, (((1,), (1,)), ((), ())), preferred_element_type=jnp.float32
        )
        grad_part = grad_part + jnp.where(
            chosen[:, None], jnp.take(input_grad, token_slot, axis=0), jnp.float32(0.0)
        )
        gate_sum, up_sum, down_sum = (
            lax.psum_scatter(
                gate_term.astype(jnp.bfloat16), "dp", scatter_dimension=0, tiled=True
            ).astype(jnp.float32),
            lax.psum_scatter(
                up_term.astype(jnp.bfloat16), "dp", scatter_dimension=0, tiled=True
            ).astype(jnp.float32),
            lax.psum_scatter(
                down_term.astype(jnp.bfloat16), "dp", scatter_dimension=1, tiled=True
            ).astype(jnp.float32),
        )
        gate_grads.append(gate_sum.astype(jnp.bfloat16))
        up_grads.append(up_sum.astype(jnp.bfloat16))
        down_grads.append(down_sum.astype(jnp.bfloat16))
    gate_grad = jnp.stack(gate_grads)
    up_grad = jnp.stack(up_grads)
    down_grad = jnp.stack(down_grads)
    token_grad = group_total(grad_part)
    return (mixed, token_grad, gate_grad, up_grad, down_grad)


def solution(mesh):
    placed = (
        P("dp", None),
        P("dp", None),
        P("dp", None),
        P(None, "dp", "fsdp"),
        P(None, "dp", "fsdp"),
        P(None, "fsdp", "dp"),
        P("dp", None),
    )
    return jax.shard_map(
        body,
        mesh=mesh,
        in_specs=placed,
        out_specs=(
            P("dp", None),
            P("dp", None),
            P(None, "dp", "fsdp"),
            P(None, "dp", "fsdp"),
            P(None, "fsdp", "dp"),
        ),
        check_vma=False,
    )
```

profile of v0, /device:TPU:4, one launch (start us, length us, event | category | flops | bytes accessed | tf_op | source)
XLA Modules:
  0.0 1003.4 jit_solution(5504983384310768062)
XLA Ops:
  19.5 5.2 gather_fusion.8
  24.7 41.6 %all-gather.21.cloned.1.call-done = bf16[1,2048,448]{1,2,0:T(8,128)(2,1)} async-done(((bf16[1,128,448]{1,2,0:T(8,128)(2,1)}), bf16[1,2048,448]{1,2,0:T(8,128)(2,1)}) %all-gather.21.cloned.1.call-update) | async-done | bytes 1835024 | tf_op jit(solution)/shard_map/all_gather | solution.py:40
  66.2 3.1 fusion.8
  69.3 52.5 %all-gather.19.cloned.1.call-done = bf16[1,2048,448]{1,2,0:T(8,128)(2,1)} async-done(((bf16[1,128,448]{1,2,0:T(8,128)(2,1)}), bf16[1,2048,448]{1,2,0:T(8,128)(2,1)}) %all-gather.19.cloned.1.call-update) | async-done | bytes 1835024 | tf_op jit(solution)/shard_map/all_gather | solution.py:39
  121.8 3.0 fusion.12
  124.9 52.0 %all-gather.23.cloned.1.call-done = bf16[1,448,2048]{2,1,0:T(8,128)(2,1)} async-done(((bf16[1,448,128]{2,1,0:T(8,128)(2,1)}), bf16[1,448,2048]{2,1,0:T(8,128)(2,1)}) %all-gather.23.cloned.1.call-update) | async-done | bytes 1835024 | tf_op jit(solution)/shard_map/all_gather | solution.py:41
  176.9 3.7 multiply_convert_fusion.2
  183.2 3.8 copy.22
  189.6 4.3 gather_fusion.6
  196.1 36.2 %all-gather.15.cloned.1.call-done = bf16[1,2048,448]{1,2,0:T(8,128)(2,1)} async-done(((bf16[1,128,448]{1,2,0:T(8,128)(2,1)}), bf16[1,2048,448]{1,2,0:T(8,128)(2,1)}) %all-gather.15.cloned.1.call-update) | async-done | bytes 1835024 | tf_op jit(solution)/shard_map/all_gather | solution.py:40
  232.3 3.0 fusion.18
  235.4 52.4 %all-gather.13.cloned.1.call-done = bf16[1,2048,448]{1,2,0:T(8,128)(2,1)} async-done(((bf16[1,128,448]{1,2,0:T(8,128)(2,1)}), bf16[1,2048,448]{1,2,0:T(8,128)(2,1)}) %all-gather.13.cloned.1.call-update) | async-done | bytes 1835024 | tf_op jit(solution)/shard_map/all_gather | solution.py:39
  287.8 3.1 fusion.22
  290.9 51.8 %all-gather.17.cloned.1.call-done = bf16[1,448,2048]{2,1,0:T(8,128)(2,1)} async-done(((bf16[1,448,128]{2,1,0:T(8,128)(2,1)}), bf16[1,448,2048]{2,1,0:T(8,128)(2,1)}) %all-gather.17.cloned.1.call-update) | async-done | bytes 1835024 | tf_op jit(solution)/shard_map/all_gather | solution.py:41
  342.7 3.3 multiply_convert_fusion.4
  348.7 2.4 copy.20
  353.2 2.5 copy.16
  361.1 2.5 copy.18
  364.5 2.4 copy.14
  369.5 3.6 gather_fusion.2
  376.3 3.6 gather_fusion.7
  382.2 3.6 gather_fusion.5
  388.9 3.6 gather_fusion.9
  392.4 9.4 fusion.1
  401.9 22.4 %reduce-scatter.29.cloned.1.call-done = bf16[128,448]{1,0:T(8,128)(2,1)} async-done(((bf16[2048,448]{1,0:T(8,128)(2,1)}), bf16[128,448]{1,0:T(8,128)(2,1)}) %reduce-scatter.29.cloned.1.call-update) | async-done | bytes 114704
  425.3 80.9 %reduce-scatter.27.cloned.1.call-done = bf16[128,448]{1,0:T(8,128)(2,1)} async-done(((bf16[2048,448]{1,0:T(8,128)(2,1)}), bf16[128,448]{1,0:T(8,128)(2,1)}) %reduce-scatter.27.cloned.1.call-update) | async-done | bytes 114704
  507.3 80.9 %reduce-scatter.23.cloned.1.call-done = bf16[128,448]{1,0:T(8,128)(2,1)} async-done(((bf16[2048,448]{1,0:T(8,128)(2,1)}), bf16[128,448]{1,0:T(8,128)(2,1)}) %reduce-scatter.23.cloned.1.call-update) | async-done | bytes 114704
  589.3 80.8 %reduce-scatter.19.cloned.1.call-done = bf16[128,448]{1,0:T(8,128)(2,1)} async-done(((bf16[2048,448]{1,0:T(8,128)(2,1)}), bf16[128,448]{1,0:T(8,128)(2,1)}) %reduce-scatter.19.cloned.1.call-update) | async-done | bytes 114704
  671.1 81.0 %reduce-scatter.25.cloned.1.call-done = bf16[128,448]{1,0:T(8,128)(2,1)} async-done(((bf16[2048,448]{1,0:T(8,128)(2,1)}), bf16[128,448]{1,0:T(8,128)(2,1)}) %reduce-scatter.25.cloned.1.call-update) | async-done | bytes 114704
  753.1 80.8 %reduce-scatter.21.cloned.1.call-done = bf16[128,448]{1,0:T(8,128)(2,1)} async-done(((bf16[2048,448]{1,0:T(8,128)(2,1)}), bf16[128,448]{1,0:T(8,128)(2,1)}) %reduce-scatter.21.cloned.1.call-update) | async-done | bytes 114704
  837.1 155.1 %all-reduce.3.cloned.1.call-done = (bf16[512,2048]{1,0:T(8,128)(2,1)}, bf16[512,2048]{1,0:T(8,128)(2,1)}) async-done(((bf16[512,2048]{1,0:T(8,128)(2,1)}, bf16[512,2048]{1,0:T(8,128)(2,1)}), (bf16[512,2048]{1,0:T(8,128)(2,1)}, bf16[512,2048]{1,0:T(8,128)(2,1)})) %all-reduce.3.cloned.1.call-update) | async-done | bytes 4194320 | tf_op jit(solution)/shard_map/psum | solution.py:24
  992.2 3.3 copy.26
  (125 shorter events, 51.1 us)
Async XLA Ops:
  7.2 10.9 %copy-start = (bf16[512,2048]{1,0:T(8,128)(2,1)S(1)}, bf16[512,2048]{1,0:T(8,128)(2,1)}, u32[]{:S(2)}) copy-start(bf16[512,2048]{1,0:T(8,128)(2,1)} %param.13) | copy-start | bytes 6291460
  7.2 7.1 copy-start.18
  7.2 8.9 copy-start.19
  7.2 59.0 %all-gather.21.cloned.1.call-start = ((), (), s32[]{:S(2)}) async-start(), calls=%async_computation.10 | async-start | bytes 1949696 | tf_op jit(solution)/shard_map/all_gather | solution.py:40
  9.1 112.8 %all-gather.19.cloned.1.call-start = ((), (), s32[]{:S(2)}) async-start(), calls=%async_computation.9 | async-start | bytes 1949696 | tf_op jit(solution)/shard_map/all_gather | solution.py:39
  10.8 166.1 %all-gather.23.cloned.1.call-start = ((), (), s32[]{:S(2)}) async-start(), calls=%async_computation.11 | async-start | bytes 1949696 | tf_op jit(solution)/shard_map/all_gather | solution.py:41
  12.5 219.8 %all-gather.15.cloned.1.call-start = ((), (), s32[]{:S(2)}) async-start(), calls=%async_computation.7 | async-start | bytes 1949696 | tf_op jit(solution)/shard_map/all_gather | solution.py:40
  13.1 274.7 %all-gather.13.cloned.1.call-start = ((), (), s32[]{:S(2)}) async-start(), calls=%async_computation.6 | async-start | bytes 1949696 | tf_op jit(solution)/shard_map/all_gather | solution.py:39
  13.7 329.0 %all-gather.17.cloned.1.call-start = ((), (), s32[]{:S(2)}) async-start(), calls=%async_computation.8 | async-start | bytes 1949696 | tf_op jit(solution)/shard_map/all_gather | solution.py:41
  14.3 410.0 %reduce-scatter.29.cloned.1.call-start = ((), (), s32[]{:S(2)}) async-start(), calls=%async_computation.17 | async-start | bytes 2228224
  176.9 4.3 copy-start.7
  187.0 319.3 %reduce-scatter.27.cloned.1.call-start = ((), (), s32[]{:S(2)}) async-start(), calls=%async_computation.16 | async-start | bytes 2228224
  189.6 42.7 %copy-start.5 = (bf16[256,2048]{1,0:T(8,128)(2,1)S(1)}, bf16[256,2048]{1,0:T(8,128)(2,1)}, u32[]{:S(2)}) copy-start(bf16[256,2048]{1,0:T(8,128)(2,1)} %gather_fusion) | copy-start | bytes 3145732
  193.9 148.7 %copy-start.6 = (bf16[256,2048]{1,0:T(8,128)(2,1)}, bf16[256,2048]{1,0:T(8,128)(2,1)S(1)}, u32[]{:S(2)}) copy-start(bf16[256,2048]{1,0:T(8,128)(2,1)S(1)} %gather_fusion.6) | copy-start | bytes 3145732
  346.0 0.7 copy-start.16
  348.7 2.5 copy-start.12
  351.2 237.1 %reduce-scatter.23.cloned.1.call-start = ((), (), s32[]{:S(2)}) async-start(), calls=%async_computation.14 | async-start | bytes 2228224
  353.2 2.6 copy-start.14
  355.8 314.3 %reduce-scatter.19.cloned.1.call-start = ((), (), s32[]{:S(2)}) async-start(), calls=%async_computation.12 | async-start | bytes 2228224
  360.2 391.8 %reduce-scatter.25.cloned.1.call-start = ((), (), s32[]{:S(2)}) async-start(), calls=%async_computation.15 | async-start | bytes 2228224
  361.1 2.7 copy-start.8
  363.6 470.3 %reduce-scatter.21.cloned.1.call-start = ((), (), s32[]{:S(2)}) async-start(), calls=%async_computation.13 | async-start | bytes 2228224
  364.5 2.7 copy-start.17
  366.9 625.3 %all-reduce.3.cloned.1.call-start = ((), (), s32[]{:S(2)}) async-start(), calls=%async_computation.18 | async-start | bytes 8388608 | tf_op jit(solution)/shard_map/psum | solution.py:24
  369.5 3.6 copy-start.15
  373.1 2.4 copy-start.4
  373.1 2.4 copy-start.13
  376.3 3.6 copy-start.11
  382.1 3.6 copy-start.9
  385.8 2.4 copy-start.3
  992.2 3.3 copy-start.2
  992.2 4.6 copy-start.1
  (1 other events, 0.7 us)
Sparse Core Ops, SparseCore 0:
  11.2 55.0 all-gather.20
  69.3 52.4 all-gather.18
  124.4 52.4 all-gather.22
  179.8 52.4 all-gather.14
  235.3 52.4 all-gather.12
  290.2 52.4 all-gather.16
  346.9 77.3 reduce-scatter.28
  428.5 77.7 reduce-scatter.26
  510.5 77.6 reduce-scatter.22
  592.3 77.7 reduce-scatter.18
  674.3 77.7 reduce-scatter.24
  756.2 77.7 reduce-scatter.20
  837.2 154.9 all-reduce.2
where the time goes:
time: 1000 us
  waiting for transfers between devices  870 us (87%)
  local copies, waits for them, and re-layouts  65.4 us (7%)
  matrix products  39.4 us (4%)
  between operations  14.3 us (1%)
  other arithmetic  13.1 us (1%)
    unnamed x19, waiting for transfers between devices  429 us
    psum x1, waiting for transfers between devices, group_total(): return lax.psum(partial_value.astype(jnp.bfloat16), 'fsdp')  155 us
    all_gather x2, waiting for transfers between devices, body(): lax.all_gather(gate_w[expert], 'dp', axis=0, tiled=True)  105 us
    all_gather x2, waiting for transfers between devices, body(): lax.all_gather(down_w[expert], 'dp', axis=1, tiled=True)  104 us
    all_gather x2, waiting for transfers between devices, body(): lax.all_gather(up_w[expert], 'dp', axis=0, tiled=True)  77.8 us
    unnamed x54, local copies, waits for them, and re-layouts  28.4 us
  transfers between devices with their start and end apart: 13, of which 13 were waited for; matrix products, arithmetic and copies ran while one was open for 11% of the time, Pallas kernels for 0%

commit v1 on v0

--- a/solution.py
+++ b/solution.py
@@ -21,7 +21,7 @@
 
 
 def group_total(partial_value):
-    return lax.psum(partial_value.astype(jnp.bfloat16), "fsdp")
+    return jnp.sum(lax.all_gather(partial_value.astype(jnp.bfloat16), "fsdp"), axis=0)
 
 
 def body(tokens, expert_ids, route_probs, gate_w, up_w, down_w, out_grad):

time: 1000 us -> 1570 us (1.57)
  waiting for transfers between devices: 870 us -> 1410 us
  other arithmetic: 13.1 us -> 39.3 us
    all_gather x0 -> x2, waiting for transfers between devices: none -> 694 us  [group_total(): lax.all_gather(partial_value.astype(jnp.bfloat16), 'fsdp')]
    psum x1 -> x0, waiting for transfers between devices: 155 us -> none  [group_total(): return lax.psum(partial_value.astype(jnp.bfloat16), 'fsdp')]
    reduce_sum x0 -> x2, other arithmetic: none -> 26.2 us  [group_total(): jnp.sum(lax.all_gather(partial_value.astype(jnp.bfloat16), 'fsdp'), axis=0)]
    unnamed x19 -> x20, waiting for transfers between devices: 429 us -> 428 us
  transfers between devices with their start and end apart: 13 -> 14, of which waited for: 13 -> 14; matrix products, arithmetic and copies ran while one was open for 11% -> 8% of each run, Pallas kernels for 0% -> 0%
where the time goes in v1:
time: 1570 us; the launch traced here: 1560 us
  waiting for transfers between devices  1410 us (90%)
  local copies, waits for them, and re-layouts  60.7 us (4%)
  matrix products  39.4 us (3%)
  other arithmetic  39.3 us (3%)
    all_gather x2, waiting for transfers between devices, group_total(): lax.all_gather(partial_value.astype(jnp.bfloat16), 'fsdp')  694 us
    unnamed x20, waiting for transfers between devices  428 us
    all_gather x2, waiting for transfers between devices, body(): lax.all_gather(gate_w[expert], 'dp', axis=0, tiled=True)  105 us
    all_gather x2, waiting for transfers between devices, body(): lax.all_gather(down_w[expert], 'dp', axis=1, tiled=True)  104 us
    all_gather x2, waiting for transfers between devices, body(): lax.all_gather(up_w[expert], 'dp', axis=0, tiled=True)  77.8 us
  transfers between devices with their start and end apart: 14, of which 14 were waited for; matrix products, arithmetic and copies ran while one was open for 8% of the time, Pallas kernels for 0%

profile of v1, /device:TPU:4, one launch (start us, length us, event | category | flops | bytes accessed | tf_op | source)
XLA Modules:
  0.0 1564.2 jit_solution(10778134750302694187)
XLA Ops:
  19.4 5.2 gather_fusion.8
  24.6 41.6 %all-gather.25.cloned.1.call-done = bf16[1,2048,448]{1,2,0:T(8,128)(2,1)} async-done(((bf16[1,128,448]{1,2,0:T(8,128)(2,1)}), bf16[1,2048,448]{1,2,0:T(8,128)(2,1)}) %all-gather.25.cloned.1.call-update) | async-done | bytes 1835024 | tf_op jit(solution)/shard_map/all_gather | solution.py:40
  66.2 3.1 fusion.8
  69.3 52.5 %all-gather.23.cloned.1.call-done = bf16[1,2048,448]{1,2,0:T(8,128)(2,1)} async-done(((bf16[1,128,448]{1,2,0:T(8,128)(2,1)}), bf16[1,2048,448]{1,2,0:T(8,128)(2,1)}) %all-gather.23.cloned.1.call-update) | async-done | bytes 1835024 | tf_op jit(solution)/shard_map/all_gather | solution.py:39
  121.8 3.0 fusion.12
  124.9 52.0 %all-gather.27.cloned.1.call-done = bf16[1,448,2048]{2,1,0:T(8,128)(2,1)} async-done(((bf16[1,448,128]{2,1,0:T(8,128)(2,1)}), bf16[1,448,2048]{2,1,0:T(8,128)(2,1)}) %all-gather.27.cloned.1.call-update) | async-done | bytes 1835024 | tf_op jit(solution)/shard_map/all_gather | solution.py:41
  176.9 3.7 multiply_convert_fusion.2
  183.2 3.8 copy.22
  189.6 4.3 gather_fusion.6
  196.1 36.2 %all-gather.19.cloned.1.call-done = bf16[1,2048,448]{1,2,0:T(8,128)(2,1)} async-done(((bf16[1,128,448]{1,2,0:T(8,128)(2,1)}), bf16[1,2048,448]{1,2,0:T(8,128)(2,1)}) %all-gather.19.cloned.1.call-update) | async-done | bytes 1835024 | tf_op jit(solution)/shard_map/all_gather | solution.py:40
  232.3 3.0 fusion.18
  235.4 52.4 %all-gather.17.cloned.1.call-done = bf16[1,2048,448]{1,2,0:T(8,128)(2,1)} async-done(((bf16[1,128,448]{1,2,0:T(8,128)(2,1)}), bf16[1,2048,448]{1,2,0:T(8,128)(2,1)}) %all-gather.17.cloned.1.call-update) | async-done | bytes 1835024 | tf_op jit(solution)/shard_map/all_gather | solution.py:39
  287.8 3.1 fusion.22
  290.8 51.8 %all-gather.21.cloned.1.call-done = bf16[1,448,2048]{2,1,0:T(8,128)(2,1)} async-done(((bf16[1,448,128]{2,1,0:T(8,128)(2,1)}), bf16[1,448,2048]{2,1,0:T(8,128)(2,1)}) %all-gather.21.cloned.1.call-update) | async-done | bytes 1835024 | tf_op jit(solution)/shard_map/all_gather | solution.py:41
  342.7 3.3 multiply_convert_fusion.4
  353.2 2.5 copy.16
  361.0 2.5 copy.18
  369.5 3.6 gather_fusion.2
  376.2 3.6 gather_fusion.7
  382.1 3.6 gather_fusion.5
  388.8 3.6 gather_fusion.9
  392.4 9.4 fusion.1
  402.4 21.9 %reduce-scatter.29.cloned.1.call-done = bf16[128,448]{1,0:T(8,128)(2,1)} async-done(((bf16[2048,448]{1,0:T(8,128)(2,1)}), bf16[128,448]{1,0:T(8,128)(2,1)}) %reduce-scatter.29.cloned.1.call-update) | async-done | bytes 114704
  425.3 80.9 %reduce-scatter.27.cloned.1.call-done = bf16[128,448]{1,0:T(8,128)(2,1)} async-done(((bf16[2048,448]{1,0:T(8,128)(2,1)}), bf16[128,448]{1,0:T(8,128)(2,1)}) %reduce-scatter.27.cloned.1.call-update) | async-done | bytes 114704
  507.3 81.0 %reduce-scatter.23.cloned.1.call-done = bf16[128,448]{1,0:T(8,128)(2,1)} async-done(((bf16[2048,448]{1,0:T(8,128)(2,1)}), bf16[128,448]{1,0:T(8,128)(2,1)}) %reduce-scatter.23.cloned.1.call-update) | async-done | bytes 114704
  589.3 80.7 %reduce-scatter.19.cloned.1.call-done = bf16[128,448]{1,0:T(8,128)(2,1)} async-done(((bf16[2048,448]{1,0:T(8,128)(2,1)}), bf16[128,448]{1,0:T(8,128)(2,1)}) %reduce-scatter.19.cloned.1.call-update) | async-done | bytes 114704
  671.0 80.9 %reduce-scatter.25.cloned.1.call-done = bf16[128,448]{1,0:T(8,128)(2,1)} async-done(((bf16[2048,448]{1,0:T(8,128)(2,1)}), bf16[128,448]{1,0:T(8,128)(2,1)}) %reduce-scatter.25.cloned.1.call-update) | async-done | bytes 114704
  753.0 80.8 %reduce-scatter.21.cloned.1.call-done = bf16[128,448]{1,0:T(8,128)(2,1)} async-done(((bf16[2048,448]{1,0:T(8,128)(2,1)}), bf16[128,448]{1,0:T(8,128)(2,1)}) %reduce-scatter.21.cloned.1.call-update) | async-done | bytes 114704
  837.0 353.7 %all-gather.31.cloned.1.call-done = bf16[8192,2048]{1,0:T(8,128)(2,1)} async-done(((bf16[512,2048]{1,0:T(8,128)(2,1)}), bf16[8192,2048]{1,0:T(8,128)(2,1)}) %all-gather.31.cloned.1.call-update) | async-done | bytes 33554448 | tf_op jit(solution)/shard_map/all_gather | solution.py:24
  1190.7 13.1 reduce_sum.65
  1203.7 340.7 %all-gather.29.cloned.1.call-done = bf16[8192,2048]{1,0:T(8,128)(2,1)} async-done(((bf16[512,2048]{1,0:T(8,128)(2,1)}), bf16[8192,2048]{1,0:T(8,128)(2,1)}) %all-gather.29.cloned.1.call-update) | async-done | bytes 33554448 | tf_op jit(solution)/shard_map/all_gather | solution.py:24
  1544.4 13.2 reduce_sum.64
  (126 shorter events, 55.2 us)
Async XLA Ops:
  7.2 10.9 copy-start
  7.2 7.1 copy-start.17
  7.2 8.9 copy-start.18
  7.2 59.0 %all-gather.25.cloned.1.call-start = ((), (), s32[]{:S(2)}) async-start(), calls=%async_computation.10 | async-start | bytes 1949696 | tf_op jit(solution)/shard_map/all_gather | solution.py:40
  9.1 112.8 %all-gather.23.cloned.1.call-start = ((), (), s32[]{:S(2)}) async-start(), calls=%async_computation.9 | async-start | bytes 1949696 | tf_op jit(solution)/shard_map/all_gather | solution.py:39
  10.8 166.1 %all-gather.27.cloned.1.call-start = ((), (), s32[]{:S(2)}) async-start(), calls=%async_computation.11 | async-start | bytes 1949696 | tf_op jit(solution)/shard_map/all_gather | solution.py:41
  12.5 219.8 %all-gather.19.cloned.1.call-start = ((), (), s32[]{:S(2)}) async-start(), calls=%async_computation.7 | async-start | bytes 1949696 | tf_op jit(solution)/shard_map/all_gather | solution.py:40
  13.1 274.7 %all-gather.17.cloned.1.call-start = ((), (), s32[]{:S(2)}) async-start(), calls=%async_computation.6 | async-start | bytes 1949696 | tf_op jit(solution)/shard_map/all_gather | solution.py:39
  13.7 329.0 %all-gather.21.cloned.1.call-start = ((), (), s32[]{:S(2)}) async-start(), calls=%async_computation.8 | async-start | bytes 1949696 | tf_op jit(solution)/shard_map/all_gather | solution.py:41
  14.3 410.0 %reduce-scatter.29.cloned.1.call-start = ((), (), s32[]{:S(2)}) async-start(), calls=%async_computation.19 | async-start | bytes 2228224
  176.9 4.3 copy-start.6
  187.0 319.2 %reduce-scatter.27.cloned.1.call-start = ((), (), s32[]{:S(2)}) async-start(), calls=%async_computation.18 | async-start | bytes 2228224
  189.6 42.7 %copy-start.4 = (bf16[256,2048]{1,0:T(8,128)(2,1)S(1)}, bf16[256,2048]{1,0:T(8,128)(2,1)}, u32[]{:S(2)}) copy-start(bf16[256,2048]{1,0:T(8,128)(2,1)} %gather_fusion) | copy-start | bytes 3145732
  193.9 148.7 %copy-start.5 = (bf16[256,2048]{1,0:T(8,128)(2,1)}, bf16[256,2048]{1,0:T(8,128)(2,1)S(1)}, u32[]{:S(2)}) copy-start(bf16[256,2048]{1,0:T(8,128)(2,1)S(1)} %gather_fusion.6) | copy-start | bytes 3145732
  346.0 0.7 copy-start.15
  348.7 2.5 copy-start.11
  351.2 237.0 %reduce-scatter.23.cloned.1.call-start = ((), (), s32[]{:S(2)}) async-start(), calls=%async_computation.16 | async-start | bytes 2228224
  353.2 2.5 copy-start.13
  355.7 314.3 %reduce-scatter.19.cloned.1.call-start = ((), (), s32[]{:S(2)}) async-start(), calls=%async_computation.14 | async-start | bytes 2228224
  360.2 391.7 %reduce-scatter.25.cloned.1.call-start = ((), (), s32[]{:S(2)}) async-start(), calls=%async_computation.17 | async-start | bytes 2228224
  361.0 2.6 copy-start.7
  363.6 470.2 %reduce-scatter.21.cloned.1.call-start = ((), (), s32[]{:S(2)}) async-start(), calls=%async_computation.15 | async-start | bytes 2228224
  364.4 2.8 copy-start.16
  366.9 823.8 %all-gather.31.cloned.1.call-start = ((), (), s32[]{:S(2)}) async-start(), calls=%async_computation.13 | async-start | bytes 35651584 | tf_op jit(solution)/shard_map/all_gather | solution.py:24
  369.5 3.6 copy-start.14
  373.1 2.4 copy-start.3
  373.1 2.4 copy-start.12
  376.2 3.6 copy-start.10
  382.1 3.6 copy-start.8
  385.7 2.4 copy-start.2
  401.8 1142.6 %all-gather.29.cloned.1.call-start = ((), (), s32[]{:S(2)}) async-start(), calls=%async_computation.12 | async-start | bytes 35651584 | tf_op jit(solution)/shard_map/all_gather | solution.py:24
  1544.4 13.2 copy-start.1
  (1 other events, 0.7 us)
Sparse Core Ops, SparseCore 0:
  11.2 55.0 all-gather.24
  69.3 52.4 all-gather.22
  124.4 52.4 all-gather.26
  179.8 52.4 all-gather.18
  235.3 52.4 all-gather.16
  290.2 52.4 all-gather.20
  346.9 77.3 reduce-scatter.28
  428.5 77.6 reduce-scatter.26
  510.5 77.7 reduce-scatter.22
  592.3 77.6 reduce-scatter.18
  674.2 77.6 reduce-scatter.24
  756.0 77.7 reduce-scatter.20
  836.2 354.4 all-gather.30
  1192.9 351.4 all-gather.28
